TPU v7x, 256 devices: a whole 4x4x8 slice. The times are simulated.
256 devices in a mesh: inp: 4 (over y_hi, core), dep: 8 (over x, y_lo), out: 8 (over z).
Axes of the slice: x: 4, y: 4 (y_hi: 2, y_lo: 2; y = y_hi * 2 + y_lo), z: 8, core: 2. Of those that a mesh axis runs over, the one named last changes fastest.
Arguments:
- tokens: bfloat16 [1024, 16384], P('inp', 'out'), may hold values from -6 to 6
- gate_up_weight: bfloat16 [16384, 2, 28672], P('out', None, ('inp', 'dep')), may hold values from -0.046875 to 0.046875
- down_weight: bfloat16 [28672, 16384], P(('inp', 'dep'), 'out'), may hold values from -0.03125 to 0.03125
Outputs:
- layer_output: bfloat16 [1024, 16384], P(('inp', 'dep'), 'out')
All inputs are finite; a program needn't handle non-finite values.
Results may differ from a plain program's by a relative error of at most 0.0049.
Values may be sent and summed in bfloat16 or wider, within the bound.
A program may use at most 128 MiB of HBM per device.

v0:
```python
import jax
import jax.numpy as jnp
from jax import lax
from jax.sharding import PartitionSpec as P


def swiglu(projected):
    return (jax.nn.silu(projected[:, 0, :]) * projected[:, 1, :]).astype(jnp.bfloat16)


def shards(tokens, gate_up_weight, down_weight):
    local_width = gate_up_weight.shape[0]
    block_units = gate_up_weight.shape[2]
    flat_weight = gate_up_weight.reshape(local_width, 2 * block_units)
    projected = jnp.dot(
        lax.all_gather(tokens, "inp", axis=0, tiled=True),
        flat_weight,
        preferred_element_type=jnp.float32,
    )
    projected = projected.reshape(projected.shape[0], 2, block_units)
    totals = lax.psum(projected, "out")
    full_hidden = swiglu(totals)
    result = lax.psum_scatter(
        jnp.dot(full_hidden, down_weight, preferred_element_type=jnp.float32),
        ("inp", "dep"),
        scatter_dimension=0,
        tiled=True,
    )
    return result.astype(jnp.bfloat16)


def solution(mesh):
    placed = (P("inp", "out"), P("out", None, ("inp", "dep")), P(("inp", "dep"), "out"))
    return jax.shard_map(
        shards, mesh=mesh, in_specs=placed, out_specs=P(("inp", "dep"), "out"), check_vma=False
    )
```

profile of v0, /device:TPU:10, one launch (start us, length us, event | category | flops | bytes accessed | tf_op | source)
XLA Modules:
  0.0 443.8 jit_solution(10383628695858579418)
XLA Ops:
  6.5 0.0 all-gather.2.cloned.1.call-start
  6.5 0.7 all-gather.2.cloned.1.call-update
  7.3 0.0 all-reduce.2.cloned.1.call-start
  7.3 7.6 %copy.5 = bf16[256,8,2,896]{3,1,2,0:T(8,128)(2,1)} copy(bf16[256,8,2,896]{3,2,1,0:T(2,128)(2,1)} %bitcast.23) | data formatting | bytes 14680064
  14.9 10.5 %copy.4 = bf16[1792,2048]{1,0:T(8,128)(2,1)} copy(bf16[1792,2048]{0,1:T(8,128)(2,1)} %bitcast.22) | data formatting | bytes 14680064 | tf_op jit(solution)/shard_map/dot_general | solution.py:15
  25.4 26.8 %all-gather.2.cloned.1.call-done = bf16[1024,2048]{1,0:T(8,128)(2,1)} async-done(((bf16[256,2048]{1,0:T(8,128)(2,1)}), bf16[1024,2048]{1,0:T(8,128)(2,1)}) %all-gather.2.cloned.1.call-update) | async-done | bytes 4194320 | tf_op jit(solution)/shard_map/all_gather | solution.py:16
  52.3 14.3 %fusion = f32[1024,2,896]{2,0,1:T(8,128)} fusion(bf16[2,896,2048]{2,1,0:T(8,128)(2,1)} %bitcast.24, bf16[1024,2048]{1,0:T(8,128)(2,1)} %all-gather.2.cloned.1.call-done), kind=kOutput, calls=%fused_computation | convolution fusion | flops 7516192768 | bytes 18874368 | tf_op jit(solution)/shard_map/dot_general | solution.py:15
  66.5 0.0 all-reduce.2.cloned.1.call-update
  66.6 0.0 reduce-scatter.2.cloned.1.call-start
  66.6 168.7 %all-reduce.2.cloned.1.call-done = f32[1024,2,896]{2,0,1:T(8,128)} async-done(((f32[1024,2,896]{2,0,1:T(8,128)}), f32[1024,2,896]{2,0,1:T(8,128)}) %all-reduce.2.cloned.1.call-update) | async-done | bytes 7340048 | tf_op jit(solution)/shard_map/psum | solution.py:21
  235.3 11.9 %fusion.4 = f32[1024,2048]{1,0:T(8,128)} fusion(bf16[896,2048]{1,0:T(8,128)(2,1)} %param.5, f32[1024,2,896]{2,0,1:T(8,128)} %all-reduce.2.cloned.1.call-done), kind=kOutput, calls=%fused_computation.6 | convolution fusion | flops 3763601408 | bytes 19398656 | tf_op jit(solution)/shard_map/dot_general | solution.py:24
  247.3 0.0 reduce-scatter.2.cloned.1.call-update
  247.3 188.3 %reduce-scatter.2.cloned.1.call-done = f32[32,2048]{1,0:T(8,128)} async-done(((f32[1024,2048]{1,0:T(8,128)}), f32[32,2048]{1,0:T(8,128)}) %reduce-scatter.2.cloned.1.call-update) | async-done | bytes 262160 | tf_op jit(solution)/shard_map/reduce_scatter | solution.py:23
  435.6 1.6 convert_element_type.7
Async XLA Ops:
  6.5 45.7 %all-gather.2.cloned.1.call-start = ((), (), s32[]{:S(2)}) async-start(), calls=%async_computation.1 | async-start | bytes 5242880 | tf_op jit(solution)/shard_map/all_gather | solution.py:16
  7.3 228.1 %all-reduce.2.cloned.1.call-start = ((), (), s32[]{:S(2)}) async-start(), calls=%async_computation.2 | async-start | bytes 14680064 | tf_op jit(solution)/shard_map/psum | solution.py:21
  66.6 369.1 %reduce-scatter.2.cloned.1.call-start = ((), (), s32[]{:S(2)}) async-start(), calls=%async_computation.3 | async-start | bytes 8650752 | tf_op jit(solution)/shard_map/reduce_scatter | solution.py:23
Sparse Core Ops, SparseCore 0:
  9.2 43.0 all-gather.1
  66.7 168.5 all-reduce.1
  247.4 188.1 reduce-scatter.1
where the time goes:
time: 444 us
  waiting for transfers between devices  385 us (87%)
  matrix products  26.2 us (6%)
  local copies, waits for them, and re-layouts  18.1 us (4%)
  between operations  13.1 us (3%)
    reduce_scatter x1, waiting for transfers between devices, shards(): lax.psum_scatter(jnp.dot(full_hidden, down_weight, preferred_element_type...  188 us
    psum x1, waiting for transfers between devices, shards(): totals = lax.psum(projected, 'out')  169 us
    all_gather x1, waiting for transfers between devices, shards(): lax.all_gather(tokens, 'inp', axis=0, tiled=True)  26.8 us
    dot_general x1, matrix products, shards(): jnp.dot(lax.all_gather(tokens, 'inp', axis=0, tiled=True), flat_weight, p...  14.3 us
    dot_general x1, matrix products, shards(): jnp.dot(full_hidden, down_weight, preferred_element_type=jnp.float32)  11.9 us
    dot_general x1, local copies, waits for them, and re-layouts, shards(): jnp.dot(lax.all_gather(tokens, 'inp', axis=0, tiled=True), flat_weight, p...  10.5 us
  transfers between devices with their start and end apart: 3, of which 3 were waited for; matrix products, arithmetic and copies ran while one was open for 4% of the time, Pallas kernels for 0%

commit v1 on v0

--- a/solution.py
+++ b/solution.py
@@ -18,7 +18,7 @@
         preferred_element_type=jnp.float32,
     )
     projected = projected.reshape(projected.shape[0], 2, block_units)
-    totals = lax.psum(projected, "out")
+    totals = lax.all_gather(projected, "out").sum(axis=0)
     full_hidden = swiglu(totals)
     result = lax.psum_scatter(
         jnp.dot(full_hidden, down_weight, preferred_element_type=jnp.float32),

time: 444 us -> 864 us (1.95)
  waiting for transfers between devices: 385 us -> 782 us
  other arithmetic: 1.62 us -> 23.5 us
    all_gather x0 -> x1, waiting for transfers between devices: none -> 566 us  [shards(): totals = lax.all_gather(projected, 'out').sum(axis=0)]
    psum x1 -> x0, waiting for transfers between devices: 169 us -> none  [shards(): totals = lax.psum(projected, 'out')]
    reduce_sum x0 -> x1, other arithmetic: none -> 21.9 us  [shards(): totals = lax.all_gather(projected, 'out').sum(axis=0)]
  transfers between devices with their start and end apart: 3 -> 3, of which waited for: 3 -> 3; matrix products, arithmetic and copies ran while one was open for 4% -> 2% of each run, Pallas kernels for 0% -> 0%
where the time goes in v1:
time: 864 us; the launch traced here: 863 us
  waiting for transfers between devices  782 us (91%)
  matrix products  26.1 us (3%)
  other arithmetic  23.5 us (3%)
  local copies, waits for them, and re-layouts  18.1 us (2%)
  between operations  13.1 us (2%)
    all_gather x1, waiting for transfers between devices, shards(): totals = lax.all_gather(projected, 'out').sum(axis=0)  566 us
    reduce_scatter x1, waiting for transfers between devices, shards(): lax.psum_scatter(jnp.dot(full_hidden, down_weight, preferred_element_type...  188 us
    all_gather x1, waiting for transfers between devices, shards(): lax.all_gather(tokens, 'inp', axis=0, tiled=True)  26.8 us
    reduce_sum x1, other arithmetic, shards(): totals = lax.all_gather(projected, 'out').sum(axis=0)  21.9 us
  transfers between devices with their start and end apart: 3, of which 3 were waited for; matrix products, arithmetic and copies ran while one was open for 2% of the time, Pallas kernels for 0%

profile of v1, /device:TPU:10, one launch (start us, length us, event | category | flops | bytes accessed | tf_op | source)
XLA Modules:
  0.0 863.1 jit_solution(13905271145227306760)
XLA Ops:
  6.5 0.0 all-gather.4.cloned.1.call-start
  6.5 0.7 all-gather.4.cloned.1.call-update
  7.3 0.0 all-gather.6.cloned.1.call-start
  7.3 7.6 copy.7
  14.9 10.5 %copy.6 = bf16[1792,2048]{1,0:T(8,128)(2,1)} copy(bf16[1792,2048]{0,1:T(8,128)(2,1)} %bitcast.24) | data formatting | bytes 14680064 | tf_op jit(solution)/shard_map/dot_general | solution.py:15
  25.4 26.8 %all-gather.4.cloned.1.call-done = bf16[1024,2048]{1,0:T(8,128)(2,1)} async-done(((bf16[256,2048]{1,0:T(8,128)(2,1)}), bf16[1024,2048]{1,0:T(8,128)(2,1)}) %all-gather.4.cloned.1.call-update) | async-done | bytes 4194320 | tf_op jit(solution)/shard_map/all_gather | solution.py:16
  52.3 14.2 %fusion = f32[1024,2,896]{2,0,1:T(8,128)} fusion(bf16[2,896,2048]{2,1,0:T(8,128)(2,1)} %bitcast.26, bf16[1024,2048]{1,0:T(8,128)(2,1)} %all-gather.4.cloned.1.call-done), kind=kOutput, calls=%fused_computation | convolution fusion | flops 7516192768 | bytes 18874368 | tf_op jit(solution)/shard_map/dot_general | solution.py:15
  66.4 0.0 all-gather.6.cloned.1.call-update
  66.5 0.0 reduce-scatter.2.cloned.1.call-start
  66.5 566.4 %all-gather.6.cloned.1.call-done = f32[8192,2,896]{2,0,1:T(8,128)} async-done(((f32[1024,2,896]{2,0,1:T(8,128)}), f32[8192,2,896]{2,0,1:T(8,128)}) %all-gather.6.cloned.1.call-update) | async-done | bytes 58720272 | tf_op jit(solution)/shard_map/all_gather | solution.py:21
  632.9 21.9 %reduce_sum.9 = f32[1024,2,896]{2,0,1:T(8,128)} reduce(f32[8,1024,2,896]{3,1,0,2:T(8,128)} %bitcast.23, f32[]{:T(128)} %constant.1.clone.1), dimensions={0}, to_apply=%region_0.0 | reduce | flops 12845056 | bytes 66060292 | tf_op jit(solution)/shard_map/reduce_sum | solution.py:21
  654.9 11.9 %fusion.4 = f32[1024,2048]{1,0:T(8,128)} fusion(bf16[896,2048]{1,0:T(8,128)(2,1)} %param.5, f32[1024,2,896]{2,0,1:T(8,128)} %reduce_sum.9), kind=kOutput, calls=%fused_computation.6 | convolution fusion | flops 3763601408 | bytes 19398656 | tf_op jit(solution)/shard_map/dot_general | solution.py:24
  666.8 0.0 reduce-scatter.2.cloned.1.call-update
  666.8 188.1 %reduce-scatter.2.cloned.1.call-done = f32[32,2048]{1,0:T(8,128)} async-done(((f32[1024,2048]{1,0:T(8,128)}), f32[32,2048]{1,0:T(8,128)}) %reduce-scatter.2.cloned.1.call-update) | async-done | bytes 262160 | tf_op jit(solution)/shard_map/reduce_scatter | solution.py:23
  854.9 1.6 convert_element_type.7
Async XLA Ops:
  6.5 45.7 %all-gather.4.cloned.1.call-start = ((), (), s32[]{:S(2)}) async-start(), calls=%async_computation.1 | async-start | bytes 5242880 | tf_op jit(solution)/shard_map/all_gather | solution.py:16
  7.3 625.7 %all-gather.6.cloned.1.call-start = ((), (), s32[]{:S(2)}) async-start(), calls=%async_computation.3 | async-start | bytes 66060288 | tf_op jit(solution)/shard_map/all_gather | solution.py:21
  66.5 788.5 %reduce-scatter.2.cloned.1.call-start = ((), (), s32[]{:S(2)}) async-start(), calls=%async_computation.2 | async-start | bytes 8650752 | tf_op jit(solution)/shard_map/reduce_scatter | solution.py:23
Sparse Core Ops, SparseCore 0:
  9.2 43.0 all-gather.3
  66.6 566.2 all-gather.5
  667.0 187.9 reduce-scatter.1
